TPU v7x, 32 devices: a whole 2x2x4 slice. The times are simulated.
32 devices in a mesh: groups: 2 (over y), row: 4 (over z), col: 2 (over x), mode: 2 (over core).
Axes of the slice: x: 2, y: 2, z: 4, core: 2. Of those that a mesh axis runs over, the one named last changes fastest.
Arguments:
- object_field: float32 [2048, 2, 1024], P(('groups', 'row'), None, 'col'), parts along dimension 0, may hold values from -12 to 12
- probe_field: float32 [512, 2, 256], P('groups'), parts along dimension 0, may hold values from -5 to 5
- amplitudes: bfloat16 [128, 256, 256], P(('groups', 'row', 'col', 'mode')), parts along dimension 0
- row_offset: int32 [128], P(('groups', 'row', 'col', 'mode')), parts along dimension 0, may hold values from 0 to 768, as said below
- col_offset: int32 [128], P(('groups', 'row', 'col', 'mode')), parts along dimension 0, may hold values from 0 to 768, as said below
- counts: int32 [32], P(('groups', 'row', 'col', 'mode')), parts along dimension 0, may hold values from 1 to 4
Outputs:
- object_new: float32 [2048, 2, 1024], P(('groups', 'row', 'mode'), None, 'col'), parts along dimension 0
- probe_new: float32 [512, 2, 256], P('groups'), parts along dimension 0
There are 2 independent parts, one for each index of `groups`. A program takes and returns all parts, laid end to end along the dimension named above; each array names one. Nothing has to cross between parts.
Inputs may be any that keep to these rules, and one draw needn't show every extreme that they name: `row_offset`: slot j lies on device j div 4 of row+col+mode; its patch starts inside that device's object tile of 256 rows, on a multiple of 64, and stays inside the object. `col_offset`: its patch starts inside the device's tile of 512 columns, on a multiple of 64, and stays inside the object.
All inputs are finite; a program needn't handle non-finite values.
Results may differ from a plain program's by a relative error of at most 0.0007.
The roundings to bfloat16 on the way count: a program that leaves them out, or rounds other values in their place, can miss the bound.
Values may be sent and summed in bfloat16 or wider, within the bound.
A program may use at most 64 MiB of HBM per device.

v0:
```python
import math

import jax
import jax.numpy as jnp
from jax import lax
from jax.sharding import PartitionSpec as P

MODULUS_FLOOR = 0.5
EPSILON = 1e-05
REGULARIZER = 1.0


def passed_along(value, axis, steps):
    count = lax.axis_size(axis)
    first, last = (max(0, -steps), min(count, count - steps))
    return lax.ppermute(value, axis, [(source, source + steps) for source in range(first, last)])


def dft_table(points, sign):
    freq_index = jnp.arange(points, dtype=jnp.int32)
    product = freq_index[:, None] * freq_index[None, :] % points
    angle_grid = 2.0 * math.pi / points * product.astype(jnp.float32)
    norm_factor = 1.0 / math.sqrt(points)
    cosine = jnp.cos(angle_grid) * norm_factor
    sine_part = jnp.sin(angle_grid) * (sign * norm_factor)
    upper_rows = jnp.stack([cosine, sine_part], axis=-1)
    lower_rows = jnp.stack([-sine_part, cosine], axis=-1)
    return jnp.stack([upper_rows, lower_rows], axis=1).astype(jnp.bfloat16)


def transform(frames, dft_matrix):
    first_pass = jnp.einsum(
        "kanb,nbm->kam", dft_matrix, frames, preferred_element_type=jnp.float32
    ).astype(jnp.bfloat16)
    return jnp.einsum("kbm,lamb->kal", first_pass, dft_matrix, preferred_element_type=jnp.float32)


def frame_update(obj_patch, probe_field, amplitude, forward, inverse):
    obj_re = obj_patch[:, 0, :].astype(jnp.float32)
    obj_im = obj_patch[:, 1, :].astype(jnp.float32)
    probe_re = probe_field[:, 0, :]
    probe_im = probe_field[:, 1, :]
    exit_wave = jnp.stack(
        [probe_re * obj_re - probe_im * obj_im, probe_re * obj_im + probe_im * obj_re], axis=1
    ).astype(jnp.bfloat16)
    far_field = transform(exit_wave, forward)
    modulus = jnp.sqrt(far_field[:, 0, :] ** 2 + far_field[:, 1, :] ** 2)
    factor = amplitude.astype(jnp.float32) / jnp.maximum(modulus, MODULUS_FLOOR) - 1.0
    change = (far_field * factor[:, None, :]).astype(jnp.bfloat16)
    back_field = transform(change, inverse)
    chi_re = back_field[:, 0, :]
    chi_im = back_field[:, 1, :]
    obj_step = jnp.stack(
        [probe_re * chi_re + probe_im * chi_im, probe_re * chi_im - probe_im * chi_re], axis=1
    )
    grad_re = obj_re * chi_re + obj_im * chi_im
    grad_im = obj_re * chi_im - obj_im * chi_re
    weight = obj_re * obj_re + obj_im * obj_im
    return (obj_step, grad_re, grad_im, weight)


def body(object_field, probe_field, amplitudes, row_offset, col_offset, counts):
    tile_rows, _, tile_cols = object_field.shape
    frame_size = probe_field.shape[0]
    forward = dft_table(frame_size, 1.0)
    inverse = dft_table(frame_size, -1.0)
    object_half = object_field.astype(jnp.bfloat16)
    below_rows = passed_along(object_half, "row", -1)
    tall_block = jnp.concatenate([object_half, below_rows], axis=0)
    right_part = passed_along(tall_block[:, :, :frame_size], "col", -1)
    extended = jnp.concatenate([tall_block, right_part], axis=2)
    top_anchor = lax.axis_index("row") * tile_rows
    left_anchor = lax.axis_index("col") * tile_cols

    def absorb(state_now, amplitude, top_row, left_col):
        update_sum, grad_re, grad_im, weight_sum = state_now
        start = (top_row - top_anchor, jnp.int32(0), left_col - left_anchor)
        obj_patch = lax.dynamic_slice(extended, start, (frame_size, 2, frame_size))
        obj_step, part_re, part_im, weight = frame_update(
            obj_patch, probe_field, amplitude, forward, inverse
        )
        current = lax.dynamic_slice(update_sum, start, (frame_size, 2, frame_size))
        update_sum = lax.dynamic_update_slice(update_sum, current + obj_step, start)
        return (update_sum, grad_re + part_re, grad_im + part_im, weight_sum + weight)

    zero_frame = jnp.zeros((frame_size, frame_size), jnp.float32)
    initial = (jnp.zeros(extended.shape, jnp.float32), zero_frame, zero_frame, zero_frame)

    def own_turn(position, state_now):
        return absorb(state_now, amplitudes[position], row_offset[position], col_offset[position])

    final_state = lax.fori_loop(0, counts[0], own_turn, initial)
    update_sum, grad_re, grad_im, weight_sum = final_state
    received = passed_along(update_sum[:, :, tile_cols:], "col", 1)
    narrow_block = update_sum[:, :, :tile_cols].at[:, :, :frame_size].add(received)
    received = passed_along(narrow_block[tile_rows:], "row", 1)
    owned_tile = narrow_block[:tile_rows].at[:frame_size].add(received)
    mode_share = lax.psum_scatter(owned_tile, "mode", scatter_dimension=0, tiled=True)
    share_rows = mode_share.shape[0]
    rows_here = lax.dynamic_slice_in_dim(
        object_field, lax.axis_index("mode") * share_rows, share_rows, 0
    )
    probe_peak = jnp.max(probe_field[:, 0, :] ** 2 + probe_field[:, 1, :] ** 2) + EPSILON
    object_new = rows_here + mode_share / probe_peak
    total_re, total_im, total_weight = lax.psum(
        (grad_re, grad_im, weight_sum), ("row", "col", "mode")
    )
    denominator = total_weight + REGULARIZER
    probe_new = probe_field + jnp.stack([total_re / denominator, total_im / denominator], axis=1)
    return (object_new, probe_new)


def solution(mesh):
    placed = (
        P(("groups", "row"), None, "col"),
        P("groups", None, None),
        P(("groups", "row", "col", "mode"), None, None),
        P(("groups", "row", "col", "mode")),
        P(("groups", "row", "col", "mode")),
        P(("groups", "row", "col", "mode")),
    )
    return jax.shard_map(
        body,
        mesh=mesh,
        in_specs=placed,
        out_specs=(P(("groups", "row", "mode"), None, "col"), P("groups", None, None)),
        check_vma=False,
    )
```

profile of v0, /device:TPU:29, one launch (start us, length us, event | category | flops | bytes accessed | tf_op | source)
XLA Modules:
  0.0 396.3 jit_solution(11456768327711181278)
XLA Ops:
  7.2 1.4 copy.25
  8.6 2.1 collective-permute-start
  12.7 8.5 %collective-permute-done = bf16[256,2,512]{0,2,1:T(8,128)(2,1)S(1)} collective-permute-done((bf16[256,2,512]{0,2,1:T(8,128)(2,1)S(1)}, bf16[256,2,512]{0,2,1:T(8,128)(2,1)S(1)}, u32[]{:S(2)}, u32[]{:S(2)}) %collective-permute-start) | collective-permute-done | bytes 524320 | tf_op jit(solution)/shard_map/ppermute | solution.py:16
  21.3 1.3 collective-permute-start.1
  26.1 9.1 %collective-permute-done.1 = bf16[512,2,256]{0,2,1:T(8,128)(2,1)} collective-permute-done((bf16[512,2,256]{0,2,1:T(8,128)(2,1)S(1)}, bf16[512,2,256]{0,2,1:T(8,128)(2,1)}, u32[]{:S(2)}, u32[]{:S(2)}) %collective-permute-start.1) | collective-permute-done | bytes 524320 | tf_op jit(solution)/shard_map/ppermute | solution.py:16
  35.2 2.3 pad_maximum_fusion
  39.0 2.5 broadcast_in_dim.4.clone
  41.4 24.6 %while.21 = (s32[]{:T(128)}, f32[512,2,768]{2,1,0:T(2,128)}, f32[256,256]{0,1:T(8,128)}, f32[256,256]{0,1:T(8,128)}, f32[256,256]{0,1:T(8,128)S(1)}, /*index=5*/...) while((s32[]{:T(128)}, f32[512,2,768]{2,1,0:T(2,128)}, ...), condition=%wide.region_1.2_spmd, body=%wide.region_0.1_spmd.sunk | while | flops 540606464 | bytes 14811535 | solution.py:92
  44.7 1.2 fusion.62
  48.2 1.7 constant_dynamic-slice_fusion.2
  50.6 2.3 fusion.64
  53.0 12.5 %dynamic_update_slice.7 = f32[512,2,768]{2,1,0:T(2,128)} dynamic-update-slice(f32[512,2,768]{2,1,0:T(2,128)} %get-tuple-element.454, f32[256,2,256]{2,1,0:T(2,128)S(1)} %copy.53, s32[]{:T(128)S(6)} %select_n.96, s32[]{:T(128)} %constant.133.clone.1..sunk, s32[]{:T(128)S(6)} %select_n.97) | dynamic-update-slice | bytes 1048580 | tf_op jit(solution)/shard_map/while/body/dynamic_update_slice | solution.py:83
  66.1 1.6 slice.116
  67.7 33.8 %collective-permute-start.2 = (f32[512,2,256]{2,1,0:T(2,128)S(1)}, f32[512,2,256]{2,1,0:T(2,128)S(1)}, u32[]{:S(2)}, u32[]{:S(2)}) collective-permute-start(f32[512,2,256]{2,1,0:T(2,128)S(1)} %slice.116), channel_id=1, source_target_pairs={{0,2},{1,3},{4,6},{5,7},{8,10},{9,11},{12,14},{13,15},{16,18},{17,... | collective-permute-start | bytes 3145736 | tf_op jit(solution)/shard_map/ppermute | solution.py:16
  101.5 2.3 slice.114
  103.8 9.1 %collective-permute-done.2 = f32[512,2,256]{2,1,0:T(2,128)S(1)} collective-permute-done((f32[512,2,256]{2,1,0:T(2,128)S(1)}, f32[512,2,256]{2,1,0:T(2,128)S(1)}, u32[]{:S(2)}, u32[]{:S(2)}) %collective-permute-start.2) | collective-permute-done | bytes 1048608 | tf_op jit(solution)/shard_map/ppermute | solution.py:16
  113.0 1.9 add_dynamic-update-slice_fusion
  114.9 1.4 slice.126
  116.3 1.3 collective-permute-start.3
  120.2 12.9 %collective-permute-done.3 = f32[256,2,512]{2,1,0:T(2,128)} collective-permute-done((f32[256,2,512]{2,1,0:T(2,128)}, f32[256,2,512]{2,1,0:T(2,128)}, u32[]{:S(2)}, u32[]{:S(2)}) %collective-permute-start.3) | collective-permute-done | bytes 1048608 | tf_op jit(solution)/shard_map/ppermute | solution.py:16
  133.1 2.8 slice_add_fusion
  138.9 223.9 %all-reduce.7.cloned.1.call-done = (f32[256,256]{1,0:T(8,128)}, f32[256,256]{1,0:T(8,128)}, f32[256,256]{1,0:T(8,128)}) async-done(((f32[256,256]{1,0:T(8,128)}, f32[256,256]{1,0:T(8,128)}, f32[256,256]{1,0:T(8,128)}), (f32[256,256]{1,0:T(8,128)}, f32[256,256]{1,0:T(8,128)}, f32[256,256]{1,0:T(8,128)})) %all-reduce.7.cloned.1.call-update) | async-done | bytes 786448 | tf_op jit(solution)/shard_map/psum | solution.py:105
  365.3 22.1 %all-reduce.5.cloned.1.call-done = f32[256,2,512]{2,1,0:T(2,128)} async-done(((f32[256,2,512]{2,1,0:T(2,128)}), f32[256,2,512]{2,1,0:T(2,128)}) %all-reduce.5.cloned.1.call-update) | async-done | bytes 1048592
  387.4 2.1 divide_add_fusion
  (49 shorter events, 17.9 us)
Async XLA Ops:
  7.2 16.5 %copy-start.2 = (f32[256,2,256]{2,1,0:T(2,128)S(1)}, f32[256,2,256]{2,1,0:T(2,128)}, u32[]{:S(2)}) copy-start(f32[256,2,256]{2,1,0:T(2,128)} %param.15) | copy-start | bytes 1572868
  7.2 355.6 %all-reduce.7.cloned.1.call-start = ((), (), s32[]{:S(2)}) async-start(), calls=%async_computation.1 | async-start | bytes 1572864 | tf_op jit(solution)/shard_map/psum | solution.py:105
  8.6 12.7 %collective-permute-start = (bf16[256,2,512]{0,2,1:T(8,128)(2,1)S(1)}, bf16[256,2,512]{0,2,1:T(8,128)(2,1)S(1)}, u32[]{:S(2)}, u32[]{:S(2)}) collective-permute-start(bf16[256,2,512]{0,2,1:T(8,128)(2,1)S(1)} %copy.25), channel_id=1, source_target_pairs={{4,0},{8,4},{12,8},{5,1},{9,5},{13,9},{6,2},{10,6},{14,10},{7,3},{... | collective-permute-start | bytes 1572872 | tf_op jit(solution)/shard_map/ppermute | solution.py:16
  21.3 13.9 %collective-permute-start.1 = (bf16[512,2,256]{0,2,1:T(8,128)(2,1)S(1)}, bf16[512,2,256]{0,2,1:T(8,128)(2,1)}, u32[]{:S(2)}, u32[]{:S(2)}) collective-permute-start(bf16[512,2,256]{0,2,1:T(8,128)(2,1)S(1)} %pad_maximum_fusion.1), channel_id=1, source_target_pairs={{2,0},{3,1},{6,4},{7,5},{10,8},{11,9},{14,12},{15,13},{18,16},{19,... | collective-permute-start | bytes 1572872 | tf_op jit(solution)/shard_map/ppermute | solution.py:16
  26.0 15.4 %copy-start.5 = (s32[4]{0:T(128)S(1)}, s32[4]{0:T(128)}, u32[]{:S(2)}) copy-start(s32[4]{0:T(128)} %param.17) | copy-start | bytes 52
  26.0 15.4 %copy-start.6 = (s32[4]{0:T(128)S(1)}, s32[4]{0:T(128)}, u32[]{:S(2)}) copy-start(s32[4]{0:T(128)} %param.18) | copy-start | bytes 52
  67.7 45.3 %collective-permute-start.2 = (f32[512,2,256]{2,1,0:T(2,128)S(1)}, f32[512,2,256]{2,1,0:T(2,128)S(1)}, u32[]{:S(2)}, u32[]{:S(2)}) collective-permute-start(f32[512,2,256]{2,1,0:T(2,128)S(1)} %slice.116), channel_id=1, source_target_pairs={{0,2},{1,3},{4,6},{5,7},{8,10},{9,11},{12,14},{13,15},{16,18},{17,... | collective-permute-start | bytes 3145736 | tf_op jit(solution)/shard_map/ppermute | solution.py:16
  103.8 14.6 %copy-start.1 = (f32[256,256]{0,1:T(8,128)S(1)}, f32[256,256]{0,1:T(8,128)}, u32[]{:S(2)}) copy-start(f32[256,256]{0,1:T(8,128)} %get-tuple-element.226) | copy-start | bytes 786436
  103.8 15.4 %copy-start = (f32[256,256]{0,1:T(8,128)S(1)}, f32[256,256]{0,1:T(8,128)}, u32[]{:S(2)}) copy-start(f32[256,256]{0,1:T(8,128)} %get-tuple-element.228) | copy-start | bytes 786436
  116.3 16.8 %collective-permute-start.3 = (f32[256,2,512]{2,1,0:T(2,128)}, f32[256,2,512]{2,1,0:T(2,128)}, u32[]{:S(2)}, u32[]{:S(2)}) collective-permute-start(f32[256,2,512]{2,1,0:T(2,128)} %slice.126), channel_id=1, source_target_pairs={{0,4},{4,8},{8,12},{1,5},{5,9},{9,13},{2,6},{6,10},{10,14},{3,7},{... | collective-permute-start | bytes 3145736 | tf_op jit(solution)/shard_map/ppermute | solution.py:16
  118.4 17.5 %copy-start.3 = (f32[256,2,256]{2,1,0:T(2,128)S(1)}, f32[256,2,256]{2,1,0:T(2,128)}, u32[]{:S(2)}) copy-start(f32[256,2,256]{2,1,0:T(2,128)} %param.15) | copy-start | bytes 1572868
  119.3 18.4 %copy-start.7 = (u32[32]{0:T(128)S(1)}, u32[32]{0:T(128)}, u32[]{:S(2)}) copy-start(u32[32]{0:T(128)} %constant.152) | copy-start | bytes 388
  120.1 267.3 %all-reduce.5.cloned.1.call-start = ((), (), s32[]{:S(2)}) async-start(), calls=%async_computation | async-start | bytes 2097152
  135.8 251.6 %copy-start.4 = (f32[256,2,512]{2,1,0:T(2,128)S(1)}, f32[256,2,512]{2,1,0:T(2,128)}, u32[]{:S(2)}) copy-start(f32[256,2,512]{2,1,0:T(2,128)} %param.14) | copy-start | bytes 3145732
Sparse Core Ops, SparseCore 0:
  120.2 242.5 all-reduce.6
  365.3 22.0 all-reduce.4
where the time goes:
time: 395 us; the launch traced here: 396 us
  waiting for transfers between devices  286 us (72%)
  starting transfers between devices  38.6 us (10%)
  local copies, waits for them, and re-layouts  31.1 us (8%)
  other arithmetic  21.4 us (5%)
  between operations  15.6 us (4%)
    psum x1, waiting for transfers between devices, body(): lax.psum((grad_re, grad_im, weight_sum), ('row', 'col', 'mode'))  224 us
    ppermute x4, waiting for transfers between devices, passed_along(): lax.ppermute(value, axis, [(source, source + steps) for source in range(f...  39.7 us
    ppermute x4, starting transfers between devices, passed_along(): lax.ppermute(value, axis, [(source, source + steps) for source in range(f...  38.5 us
    unnamed x3, waiting for transfers between devices  22.2 us
    dynamic_update_slice x2, local copies, waits for them, and re-layouts, absorb(): update_sum = lax.dynamic_update_slice(update_sum, current + obj_step, start)  12.7 us
  transfers between devices with their start and end apart: 6, of which 6 were waited for; matrix products, arithmetic and copies ran while one was open for 4% of the time, Pallas kernels for 0%

commit v1 on v0

v1 whole, which is shorter than its diff:
```python
import functools
import math

import jax
import jax.numpy as jnp
import numpy as np
from jax import lax
from jax.experimental import pallas as pl
from jax.experimental.pallas import tpu as pltpu
from jax.sharding import PartitionSpec as P

FLOOR_SQUARED = 0.25
EPSILON = 1e-05
REGULARIZER = 1.0
F32 = jnp.float32
BF16 = jnp.bfloat16
MESH = pl.DeviceIdType.MESH
VMEM = pltpu.VMEM
LANES = 128
SHIFT = 64


def dft_tables(points):
    index = np.arange(points)
    product = (index[:, None] * index[None, :]) % points
    angle = (2.0 * math.pi / points) * product.astype(np.float32)
    norm = np.float32(1.0 / math.sqrt(points))
    cosine = (np.cos(angle.astype(np.float32)) * norm).astype(np.float32)
    sine = (np.sin(angle.astype(np.float32)) * norm).astype(np.float32)
    first = np.block([[cosine, sine], [-sine, cosine]])
    second = np.block([[cosine, -sine], [sine, cosine]])
    return jnp.asarray(first, BF16), jnp.asarray(second, BF16)


def greet(peers):
    barrier = pltpu.get_barrier_semaphore()
    expected = jnp.int32(0)
    for present, where in peers:
        expected = expected + present.astype(jnp.int32)

        @pl.when(present)
        def _(where=where):
            pl.semaphore_signal(barrier, inc=1, device_id=where, device_id_type=MESH)

    pl.semaphore_wait(barrier, expected)


def remote(src, dst, sems, slot, where):
    return pltpu.make_async_remote_copy(
        src_ref=src,
        dst_ref=dst,
        send_sem=sems.at[0, slot],
        recv_sem=sems.at[1, slot],
        device_id=where,
        device_id_type=MESH,
    )


def halo_kernel(rows_n, cols_n, obj_ref, ext_ref, sems):
    r = lax.axis_index("row")
    c = lax.axis_index("col")
    m = lax.axis_index("mode")
    _, tile_r, tile_c = obj_ref.shape
    half = tile_r // 2
    frame = ext_ref.shape[2] - tile_c
    has_up, has_down = r > 0, r < rows_n - 1
    has_left, has_right = c > 0, c < cols_n - 1
    sib = {"mode": 1 - m}
    up, down = {"row": r - 1}, {"row": r + 1}
    left, right = {"col": c - 1}, {"col": c + 1}
    always = m >= 0
    greet([(always, sib), (has_up, up), (has_down, down), (has_left, left), (has_right, right)])
    mine = pl.ds(pl.multiple_of(m * half, half), half)
    below = pl.ds(pl.multiple_of(tile_r + m * half, half), half)
    edge = pl.ds(tile_c, frame)
    body = pl.ds(0, tile_c)
    to_left = remote(obj_ref.at[:, mine, pl.ds(0, frame)], ext_ref.at[:, mine, edge], sems, 0, left)
    to_up = remote(obj_ref.at[:, mine, :], ext_ref.at[:, below, body], sems, 1, up)
    corner_up = remote(ext_ref.at[:, mine, edge], ext_ref.at[:, below, edge], sems, 2, up)
    swap_edge = remote(ext_ref.at[:, mine, edge], ext_ref.at[:, mine, edge], sems, 3, sib)
    swap_below = remote(ext_ref.at[:, below, body], ext_ref.at[:, below, body], sems, 4, sib)
    swap_corner = remote(ext_ref.at[:, below, edge], ext_ref.at[:, below, edge], sems, 5, sib)

    @pl.when(has_left)
    def _():
        to_left.start()

    @pl.when(has_up)
    def _():
        to_up.start()

    ext_ref[:, pl.ds(0, tile_r), body] = obj_ref[...]

    @pl.when(has_right)
    def _():
        to_left.wait_recv()

        @pl.when(has_up)
        def _():
            corner_up.start()

        swap_edge.start()

    @pl.when(has_down)
    def _():
        to_up.wait_recv()
        swap_below.start()

    @pl.when(has_right & has_down)
    def _():
        corner_up.wait_recv()
        swap_corner.start()
        swap_corner.wait()

    @pl.when(has_right)
    def _():
        swap_edge.wait()

        @pl.when(has_up)
        def _():
            corner_up.wait_send()

    @pl.when(has_down)
    def _():
        swap_below.wait()

    @pl.when(has_left)
    def _():
        to_left.wait_send()

    @pl.when(has_up)
    def _():
        to_up.wait_send()


def halo(obj, frame, rows_n, cols_n):
    planes, tile_r, tile_c = obj.shape
    return pl.pallas_call(
        functools.partial(halo_kernel, rows_n, cols_n),
        out_shape=jax.ShapeDtypeStruct((planes, tile_r + frame, tile_c + frame), BF16),
        in_specs=[pl.BlockSpec(memory_space=VMEM)],
        out_specs=pl.BlockSpec(memory_space=VMEM),
        scratch_shapes=[pltpu.SemaphoreType.DMA((2, 6))],
        compiler_params=pltpu.CompilerParams(
            collective_id=0, has_side_effects=True, vmem_limit_bytes=48 << 20
        ),
        name="halo",
    )(obj)


def frames_kernel(
    row_ref, col_ref, count_ref, ext_ref, probe_ref, amp_ref, first_ref, second_ref,
    upd_ref, sum_ref, obj, acc, tall, wide, field,
):
    frame = probe_ref.shape[1]
    ext_rows, ext_cols = ext_ref.shape[1:]
    top = lax.axis_index("row") * (ext_rows - frame)
    left = lax.axis_index("col") * (ext_cols - frame)
    step = 32
    for plane in range(2):
        for row in range(0, ext_rows, 64):
            rows = pl.ds(row, 64)
            value = ext_ref[plane, rows, :]
            obj[0, plane, rows, :] = value
            moved = pltpu.roll(value.astype(F32), ext_cols - SHIFT, 1)
            obj[1, plane, rows, :] = moved.astype(BF16)
    acc[...] = jnp.zeros_like(acc)
    sum_ref[...] = jnp.zeros_like(sum_ref)

    def one(slot, carry):
        row = row_ref[slot] - top
        col = col_ref[slot] - left
        odd = (col % LANES) // SHIFT
        cols = pl.ds(pl.multiple_of((col // LANES) * LANES, LANES), frame)
        for k in range(0, frame, step):
            rows = pl.ds(pl.multiple_of(row + k, step), step)
            o_re = obj[odd, 0, rows, cols].astype(F32)
            o_im = obj[odd, 1, rows, cols].astype(F32)
            p_re = probe_ref[0, k : k + step, :]
            p_im = probe_ref[1, k : k + step, :]
            tall[k : k + step, :] = (p_re * o_re - p_im * o_im).astype(BF16)
            tall[frame + k : frame + k + step, :] = (p_re * o_im + p_im * o_re).astype(BF16)
        half = jnp.dot(first_ref[...], tall[...], preferred_element_type=F32).astype(BF16)
        wide[:, :frame] = half[:frame]
        wide[:, frame:] = half[frame:]
        field[...] = jnp.dot(wide[...], second_ref[...], preferred_element_type=F32)
        for k in range(0, frame, step):
            f_re = field[k : k + step, :frame]
            f_im = field[k : k + step, frame:]
            amp = amp_ref[slot, k : k + step, :].astype(F32)
            power = f_re * f_re + f_im * f_im
            factor = amp * lax.rsqrt(jnp.maximum(power, FLOOR_SQUARED)) - 1.0
            tall[k : k + step, :] = (f_re * factor).astype(BF16)
            tall[frame + k : frame + k + step, :] = (f_im * factor).astype(BF16)
        half = jnp.dot(second_ref[...], tall[...], preferred_element_type=F32).astype(BF16)
        wide[:, :frame] = half[:frame]
        wide[:, frame:] = half[frame:]
        field[...] = jnp.dot(wide[...], first_ref[...], preferred_element_type=F32)
        for k in range(0, frame, step):
            rows = pl.ds(pl.multiple_of(row + k, step), step)
            here = pl.ds(k, step)
            x_re = field[k : k + step, :frame]
            x_im = field[k : k + step, frame:]
            o_re = obj[odd, 0, rows, cols].astype(F32)
            o_im = obj[odd, 1, rows, cols].astype(F32)
            p_re = probe_ref[0, k : k + step, :]
            p_im = probe_ref[1, k : k + step, :]
            acc[odd, 0, rows, cols] += p_re * x_re + p_im * x_im
            acc[odd, 1, rows, cols] += p_re * x_im - p_im * x_re
            sum_ref[0, here, :] += o_re * x_re + o_im * x_im
            sum_ref[1, here, :] += o_re * x_im - o_im * x_re
            sum_ref[2, here, :] += o_re * o_re + o_im * o_im
        return carry

    lax.fori_loop(0, count_ref[0], one, 0)
    for plane in range(2):
        for row in range(0, ext_rows, 64):
            rows = pl.ds(row, 64)
            upd_ref[plane, rows, :] = acc[0, plane, rows, :] + pltpu.roll(
                acc[1, plane, rows, :], SHIFT, 1
            )


def frames(row_offset, col_offset, counts, ext, probe, amplitudes, first, second):
    frame = probe.shape[1]
    in_vmem = pl.BlockSpec(memory_space=VMEM)
    in_smem = pl.BlockSpec(memory_space=pltpu.SMEM)
    return pl.pallas_call(
        frames_kernel,
        out_shape=(
            jax.ShapeDtypeStruct(ext.shape, F32),
            jax.ShapeDtypeStruct((3, frame, frame), F32),
        ),
        in_specs=[in_smem] * 3 + [in_vmem] * 5,
        out_specs=(in_vmem, in_vmem),
        scratch_shapes=[
            VMEM((2, *ext.shape), BF16),
            VMEM((2, *ext.shape), F32),
            VMEM((2 * frame, frame), BF16),
            VMEM((frame, 2 * frame), BF16),
            VMEM((frame, 2 * frame), F32),
        ],
        compiler_params=pltpu.CompilerParams(vmem_limit_bytes=48 << 20),
        name="frames",
    )(row_offset, col_offset, counts, ext, probe, amplitudes, first, second)


def merge_kernel(
    rows_n, cols_n, with_probe, upd_ref, sum_ref, probe_ref, share_ref, fresh_ref,
    total, got, from_left, from_up, got_sum, part, col_got, row_part, row_got, sems, psems,
):
    r = lax.axis_index("row")
    c = lax.axis_index("col")
    m = lax.axis_index("mode")
    half, tile_c = share_ref.shape[1:]
    tile_r = 2 * half
    frame = probe_ref.shape[1]
    has_up, has_down = r > 0, r < rows_n - 1
    has_left, has_right = c > 0, c < cols_n - 1
    sib = {"mode": 1 - m}
    up, down = {"row": r - 1}, {"row": r + 1}
    left, right = {"col": c - 1}, {"col": c + 1}
    always = m >= 0
    row_peers = [{"row": lax.rem(r + d, rows_n)} for d in range(1, rows_n)]
    col_peers = [{"col": lax.rem(c + d, cols_n)} for d in range(1, cols_n)]
    if with_probe:
        greet([(always, p) for p in [sib] + row_peers + col_peers])
    else:
        greet([(always, sib), (has_up, up), (has_down, down), (has_left, left), (has_right, right)])

    def block(which, base):
        return pl.ds(pl.multiple_of(which * half + base, half), half)

    top_mine, low_mine = block(m, 0), block(m, tile_r)
    top_sib, low_sib = block(1 - m, 0), block(1 - m, tile_r)
    first_cols, mid_cols, edge = pl.ds(0, frame), pl.ds(frame, tile_c - frame), pl.ds(tile_c, frame)
    pieces = [(1, edge), (1, mid_cols), (0, edge), (1, first_cols), (0, pl.ds(0, tile_c))]
    if with_probe:
        sum_rows = frame // 2
        col_rows = sum_rows // cols_n
        row_rows = col_rows // rows_n
        mine_at = m * sum_rows
        give = sum_ref.at[:, pl.ds(pl.multiple_of((1 - m) * sum_rows, sum_rows), sum_rows), :]
        swap_sum = remote(give, got_sum, psems, 0, sib)
        swap_sum.start()
    swaps = []
    for slot, (low, cols) in enumerate(pieces):
        src = upd_ref.at[:, low_sib if low else top_sib, cols]
        swaps.append(remote(src, got.at[low, :, :, cols], sems, slot, sib))
        swaps[-1].start()

    def joined(index):
        low, cols = pieces[index]
        swaps[index].wait_recv()
        total[low, :, :, cols] = upd_ref[:, low_mine if low else top_mine, cols] + got[low, :, :, cols]

    corner = remote(total.at[1, :, :, edge], from_left.at[1], sems, 5, right)
    side = remote(total.at[0, :, :, edge], from_left.at[0], sems, 6, right)
    fall_mid = remote(total.at[1, :, :, mid_cols], from_up.at[:, :, mid_cols], sems, 7, down)
    fall_first = remote(total.at[1, :, :, first_cols], from_up.at[:, :, first_cols], sems, 8, down)

    if with_probe:
        swap_sum.wait_recv()
        at = pl.ds(pl.multiple_of(mine_at, sum_rows), sum_rows)
        part[...] = sum_ref[:, at, :] + got_sum[...]
        col_copies = []
        for d in range(1, cols_n):
            there = lax.rem(c + d, cols_n)
            src = part.at[:, pl.ds(pl.multiple_of(there * col_rows, col_rows), col_rows), :]
            col_copies.append(remote(src, col_got.at[d - 1], psems, d, col_peers[d - 1]))
            col_copies[-1].start()
    joined(0)

    @pl.when(has_right)
    def _():
        corner.start()

    joined(1)

    @pl.when(has_down)
    def _():
        fall_mid.start()

    joined(2)

    @pl.when(has_right)
    def _():
        side.start()

    joined(3)
    base = cols_n
    if with_probe:
        own = part[:, pl.ds(pl.multiple_of(c * col_rows, col_rows), col_rows), :]
        for d in range(1, cols_n):
            col_copies[d - 1].wait_recv()
            own = own + col_got[d - 1]
        row_part[...] = own
        row_copies = []
        for d in range(1, rows_n):
            there = lax.rem(r + d, rows_n)
            src = row_part.at[:, pl.ds(pl.multiple_of(there * row_rows, row_rows), row_rows), :]
            row_copies.append(remote(src, row_got.at[d - 1], psems, base + d, row_peers[d - 1]))
            row_copies[-1].start()

    @pl.when(has_left)
    def _():
        corner.wait_recv()
        total[1, :, :, first_cols] += from_left[1]

    @pl.when(has_down)
    def _():
        fall_first.start()

    peak = probe_ref[0] * probe_ref[0] + probe_ref[1] * probe_ref[1]
    peak = jnp.max(peak, keepdims=True) + EPSILON
    base += rows_n
    if with_probe:
        own = row_part[:, pl.ds(pl.multiple_of(r * row_rows, row_rows), row_rows), :]
        for d in range(1, rows_n):
            row_copies[d - 1].wait_recv()
            own = own + row_got[d - 1]
        weight = own[2] + REGULARIZER
        start = mine_at + c * col_rows
        shard = pl.ds(pl.multiple_of(start + r * row_rows, row_rows), row_rows)
        fresh_ref[0, shard, :] = probe_ref[0, shard, :] + own[0] / weight
        fresh_ref[1, shard, :] = probe_ref[1, shard, :] + own[1] / weight
        spread = []
        for d in range(1, rows_n):
            ref = fresh_ref.at[:, shard, :]
            spread.append(remote(ref, ref, psems, base + d, row_peers[d - 1]))
            spread[-1].start()
        base += rows_n
        for d in range(1, rows_n):
            spread[d - 1].wait_recv()
        ref = fresh_ref.at[:, pl.ds(pl.multiple_of(start, col_rows), col_rows), :]
        for d in range(1, cols_n):
            spread.append(remote(ref, ref, psems, base + d, col_peers[d - 1]))
            spread[-1].start()
        base += cols_n
    else:
        fresh_ref[...] = jnp.zeros_like(fresh_ref)
    joined(4)

    @pl.when(has_left)
    def _():
        side.wait_recv()
        total[0, :, :, first_cols] += from_left[0]

    if with_probe:
        for d in range(1, cols_n):
            spread[rows_n - 1 + d - 1].wait_recv()
        ref = fresh_ref.at[:, pl.ds(pl.multiple_of(mine_at, sum_rows), sum_rows), :]
        last = remote(ref, ref, psems, base, sib)
        last.start()

    @pl.when(has_up)
    def _():
        fall_mid.wait_recv()
        fall_first.wait_recv()
        total[0, :, :, pl.ds(0, tile_c)] += from_up[...]

    share_ref[...] = total[0, :, :, pl.ds(0, tile_c)] / peak

    for copy in swaps:
        copy.wait_send()

    @pl.when(has_right)
    def _():
        corner.wait_send()
        side.wait_send()

    @pl.when(has_down)
    def _():
        fall_mid.wait_send()
        fall_first.wait_send()

    if with_probe:
        swap_sum.wait_send()
        for copy in col_copies + row_copies + spread:
            copy.wait_send()
        last.wait()


def merge(upd, sums, probe, tile_r, tile_c, rows_n, cols_n, with_probe):
    frame = probe.shape[1]
    half = tile_r // 2
    ext_c = tile_c + frame
    sum_rows = frame // 2
    if with_probe:
        col_rows = sum_rows // cols_n
        row_rows = col_rows // rows_n
    else:
        col_rows = row_rows = 8
    in_vmem = pl.BlockSpec(memory_space=VMEM)
    return pl.pallas_call(
        functools.partial(merge_kernel, rows_n, cols_n, with_probe),
        out_shape=(
            jax.ShapeDtypeStruct((2, half, tile_c), F32),
            jax.ShapeDtypeStruct((2, frame, frame), F32),
        ),
        in_specs=[in_vmem] * 3,
        out_specs=(in_vmem, in_vmem),
        scratch_shapes=[
            VMEM((2, 2, half, ext_c), F32),
            VMEM((2, 2, half, ext_c), F32),
            VMEM((2, 2, half, frame), F32),
            VMEM((2, half, tile_c), F32),
            VMEM((3, sum_rows, frame), F32),
            VMEM((3, sum_rows, frame), F32),
            VMEM((max(1, cols_n - 1), 3, col_rows, frame), F32),
            VMEM((3, col_rows, frame), F32),
            VMEM((max(1, rows_n - 1), 3, row_rows, frame), F32),
            pltpu.SemaphoreType.DMA((2, 9)),
            pltpu.SemaphoreType.DMA((2, 2 * rows_n + 2 * cols_n + 1)),
        ],
        compiler_params=pltpu.CompilerParams(
            collective_id=1, has_side_effects=True, vmem_limit_bytes=48 << 20
        ),
        name="merge",
    )(upd, sums, probe)


def body(rows_n, cols_n, object_field, probe_field, amplitudes, row_offset, col_offset, counts):
    tile_r, _, tile_c = object_field.shape
    frame = probe_field.shape[0]
    half = tile_r // 2
    first, second = dft_tables(frame)
    obj = jnp.moveaxis(object_field.astype(BF16), 1, 0)
    probe = jnp.moveaxis(probe_field, 1, 0)
    ext = halo(obj, frame, rows_n, cols_n)
    upd, sums = frames(row_offset, col_offset, counts, ext, probe, amplitudes, first, second)
    with_probe = frame % (2 * rows_n * cols_n * 8) == 0
    share, fresh = merge(upd, sums, probe, tile_r, tile_c, rows_n, cols_n, with_probe)
    rows_here = lax.dynamic_slice_in_dim(object_field, lax.axis_index("mode") * half, half, 0)
    object_new = rows_here + jnp.moveaxis(share, 0, 1)
    if with_probe:
        return (object_new, jnp.moveaxis(fresh, 0, 1))
    sums = lax.psum(sums, ("row", "col", "mode"))
    fresh = probe + sums[:2] / (sums[2:] + REGULARIZER)
    return (object_new, jnp.moveaxis(fresh, 0, 1))


def solution(mesh):
    split = ("groups", "row", "col", "mode")
    placed = (
        P(("groups", "row"), None, "col"),
        P("groups", None, None),
        P(split, None, None),
        P(split),
        P(split),
        P(split),
    )
    return jax.shard_map(
        functools.partial(body, mesh.shape["row"], mesh.shape["col"]),
        mesh=mesh,
        in_specs=placed,
        out_specs=(P(("groups", "row", "mode"), None, "col"), P("groups", None, None)),
        check_vma=False,
    )
```

time: 395 us -> 61.2 us (0.15)
  waiting for transfers between devices: 286 us -> 0 us
  Pallas kernels: 0 us -> 52.3 us
  starting transfers between devices: 38.6 us -> 0 us
  local copies, waits for them, and re-layouts: 31.1 us -> 7.09 us
  other arithmetic: 21.4 us -> 0.09 us
  between operations: 15.6 us -> 1.42 us
    psum x1 -> x0, waiting for transfers between devices: 224 us -> none  [body(): lax.psum((grad_re, grad_im, weight_sum), ('row', 'col', 'mode'))]
    pallas_call x0 -> x3, Pallas kernels: none -> 52.3 us  [the longest x1 35.9 us: merge(): pl.pallas_call(functools.partial(merge_kernel, rows_n, cols_n, with_probe...]
    ppermute x4 -> x0, waiting for transfers between devices: 39.7 us -> none  [passed_along(): lax.ppermute(value, axis, [(source, source + steps) for source in range(f...]
    ppermute x4 -> x0, starting transfers between devices: 38.5 us -> none  [passed_along(): lax.ppermute(value, axis, [(source, source + steps) for source in range(f...]
    unnamed x3 -> x0, waiting for transfers between devices: 22.2 us -> none
    dynamic_update_slice x2 -> x0, local copies, waits for them, and re-layouts: 12.7 us -> none  [absorb(): update_sum = lax.dynamic_update_slice(update_sum, current + obj_step, start)]
    another operation x9 -> x0, other arithmetic: 7.5 us -> none
    add x6 -> x1, other arithmetic: 7.43 us -> 0.09 us  [body(): object_new = rows_here + jnp.moveaxis(share, 0, 1)]
  transfers between devices with their start and end apart: 6 -> 0, of which waited for: 6 -> 0; matrix products, arithmetic and copies ran while one was open for 4% -> 0% of each run, Pallas kernels for 0% -> 0%
where the time goes in v1:
time: 61.2 us; the launch traced here: 60.9 us
  Pallas kernels  52.3 us (85%)
  local copies, waits for them, and re-layouts  7.09 us (12%)
  between operations  1.42 us (2%)
    pallas_call x1, Pallas kernels, merge(): pl.pallas_call(functools.partial(merge_kernel, rows_n, cols_n, with_probe...  35.9 us
    pallas_call x1, Pallas kernels, halo(): pl.pallas_call(functools.partial(halo_kernel, rows_n, cols_n), out_shape=...  9.18 us
    pallas_call x1, Pallas kernels, frames(): pl.pallas_call(frames_kernel, out_shape=(jax.ShapeDtypeStruct(ext.shape,...  7.23 us
    unnamed x19, local copies, waits for them, and re-layouts  7.09 us

profile of v1, /device:TPU:29, one launch (start us, length us, event | category | flops | bytes accessed | tf_op | source)
XLA Modules:
  0.0 60.9 jit_solution(5941484087211012100)
XLA Ops:
  0.6 0.0 copy-start.2
  0.6 0.0 copy-start.3
  0.7 0.0 copy-start.1
  0.7 0.0 copy-start.4
  0.7 0.0 copy-start.5
  0.7 1.2 %copy.17 = f32[256,2,256]{2,0,1:T(8,128)S(1)} copy(f32[256,2,256]{2,1,0:T(2,128)} %param.9) | data formatting | bytes 1048576 | tf_op args[1]
  1.9 1.4 %copy.18 = bf16[256,2,512]{2,0,1:T(8,128)(2,1)S(1)} copy(f32[256,2,512]{2,1,0:T(2,128)} %param.8) | data formatting | bytes 1572864 | tf_op args[0]
  3.3 9.2 %halo.1.ext_ref = bf16[2,512,768]{2,1,0:T(8,128)(2,1)S(1)} custom-call(bf16[2,256,512]{2,1,0:T(8,128)(2,1)S(1)} %bitcast.11), custom_call_target="tpu_custom_call" | custom-call | tf_op jit(solution)/shard_map/halo/pallas_call | solution.py:138
  13.1 0.0 copy-done.2
  13.1 0.0 copy-done.3
  13.1 0.0 copy-done.1
  13.1 0.0 copy-done.4
  13.1 0.0 copy-done.5
  13.2 0.0 copy-start.6
  13.2 7.2 %frames.1 = (f32[2,512,768]{2,1,0:T(8,128)}, f32[3,256,256]{2,1,0:T(8,128)S(1)}) custom-call(s32[4]{0:T(128)S(1)} %copy-done.4, s32[4]{0:T(128)S(1)} %copy-done.5, s32[1]{0:T(128)S(6)} %copy.19.count_ref, bf16[2,512,768]{2,1,0:T(8,128)(2,1)S(1)} %halo.1.ext_ref, f32[2,256,256]{2,1,0:T(8,128)S(1)} %bitcast.9, bf16[4,256,256]{2,1,0:T(8,128)(2,1)S(1)} %copy-done.1, ...), custom_call_target="tpu_custom_call" | custom-call | tf_op jit(solution)/shard_map/frames/pallas_call | solution.py:228
  20.4 0.0 copy-start
  20.4 1.9 %copy-done = f32[2,512,768]{2,1,0:T(8,128)S(1)} copy-done((f32[2,512,768]{2,1,0:T(8,128)S(1)}, f32[2,512,768]{2,1,0:T(8,128)}, u32[]{:S(2)}) %copy-start) | copy-done | bytes 3145752
  22.3 35.9 %merge.1 = (f32[2,128,512]{2,1,0:T(8,128)S(1)}, f32[2,256,256]{2,1,0:T(8,128)S(1)}) custom-call(f32[2,512,768]{2,1,0:T(8,128)S(1)} %copy-done, f32[3,256,256]{2,1,0:T(8,128)S(1)} %get-tuple-element.7.sum_ref, f32[2,256,256]{2,1,0:T(8,128)S(1)} %bitcast.10), custom_call_target="tpu_custom_call" | custom-call | tf_op jit(solution)/shard_map/merge/pallas_call | solution.py:435
  58.2 0.0 copy-done.6
  58.2 0.2 copy.10
  58.4 0.1 bitcast_add_fusion
  58.5 1.2 %copy.13 = f32[128,2,512]{2,1,0:T(2,128)} copy(f32[128,2,512]{2,0,1:T(8,128)S(1)} %bitcast_add_fusion) | data formatting | bytes 1048576
  59.7 1.2 %copy.14 = f32[256,2,256]{2,1,0:T(2,128)} copy(f32[256,2,256]{2,0,1:T(8,128)S(1)} %bitcast.12) | data formatting | bytes 1048576
Async XLA Ops:
  0.6 12.5 %copy-start.2 = (bf16[512,512]{1,0:T(8,128)(2,1)S(1)}, bf16[512,512]{1,0:T(8,128)(2,1)}, u32[]{:S(2)}) copy-start(bf16[512,512]{1,0:T(8,128)(2,1)} %constant.14.clone.first_ref) | copy-start | bytes 1572868
  0.6 12.5 %copy-start.3 = (bf16[512,512]{1,0:T(8,128)(2,1)S(1)}, bf16[512,512]{1,0:T(8,128)(2,1)}, u32[]{:S(2)}) copy-start(bf16[512,512]{1,0:T(8,128)(2,1)} %constant.15.clone.second_ref) | copy-start | bytes 1572868
  0.7 12.5 %copy-start.1 = (bf16[4,256,256]{2,1,0:T(8,128)(2,1)S(1)}, bf16[4,256,256]{2,1,0:T(8,128)(2,1)}, u32[]{:S(2)}) copy-start(bf16[4,256,256]{2,1,0:T(8,128)(2,1)} %amp_ref.1) | copy-start | bytes 1572868
  0.7 12.5 %copy-start.4 = (s32[4]{0:T(128)S(1)}, s32[4]{0:T(128)}, u32[]{:S(2)}) copy-start(s32[4]{0:T(128)} %row_ref.1) | copy-start | bytes 52
  0.7 12.5 %copy-start.5 = (s32[4]{0:T(128)S(1)}, s32[4]{0:T(128)}, u32[]{:S(2)}) copy-start(s32[4]{0:T(128)} %col_ref.1) | copy-start | bytes 52
  13.2 45.0 %copy-start.6 = (f32[256,2,512]{2,1,0:T(2,128)S(1)}, f32[256,2,512]{2,1,0:T(2,128)}, u32[]{:S(2)}) copy-start(f32[256,2,512]{2,1,0:T(2,128)} %param.8) | copy-start | bytes 3145732
  20.4 1.9 %copy-start = (f32[2,512,768]{2,1,0:T(8,128)S(1)}, f32[2,512,768]{2,1,0:T(8,128)}, u32[]{:S(2)}) copy-start(f32[2,512,768]{2,1,0:T(8,128)} %get-tuple-element.6.upd_ref) | copy-start | bytes 9437188

commit v2 on v1

--- a/solution.py
+++ b/solution.py
@@ -56,13 +56,14 @@
     )
 
 
-def halo_kernel(rows_n, cols_n, obj_ref, ext_ref, sems):
+def halo_kernel(rows_n, cols_n, field_ref, probe_ref, obj_ref, planes_ref, acc_ref, sems):
     r = lax.axis_index("row")
     c = lax.axis_index("col")
     m = lax.axis_index("mode")
-    _, tile_r, tile_c = obj_ref.shape
-    half = tile_r // 2
-    frame = ext_ref.shape[2] - tile_c
+    tile_r, _, tile_c = field_ref.shape
+    frame = probe_ref.shape[0]
+    half, reach = tile_r // 2, frame - SHIFT
+    low = reach // 2
     has_up, has_down = r > 0, r < rows_n - 1
     has_left, has_right = c > 0, c < cols_n - 1
     sib = {"mode": 1 - m}
@@ -70,51 +71,82 @@
     left, right = {"col": c - 1}, {"col": c + 1}
     always = m >= 0
     greet([(always, sib), (has_up, up), (has_down, down), (has_left, left), (has_right, right)])
+    ext = obj_ref.at[0]
     mine = pl.ds(pl.multiple_of(m * half, half), half)
-    below = pl.ds(pl.multiple_of(tile_r + m * half, half), half)
+    other = pl.ds(pl.multiple_of((1 - m) * half, half), half)
+    lift = pl.ds(pl.multiple_of(m * low, 32), low)
+    below = pl.ds(pl.multiple_of(tile_r + m * low, 32), low)
     edge = pl.ds(tile_c, frame)
     body = pl.ds(0, tile_c)
-    to_left = remote(obj_ref.at[:, mine, pl.ds(0, frame)], ext_ref.at[:, mine, edge], sems, 0, left)
-    to_up = remote(obj_ref.at[:, mine, :], ext_ref.at[:, below, body], sems, 1, up)
-    corner_up = remote(ext_ref.at[:, mine, edge], ext_ref.at[:, below, edge], sems, 2, up)
-    swap_edge = remote(ext_ref.at[:, mine, edge], ext_ref.at[:, mine, edge], sems, 3, sib)
-    swap_below = remote(ext_ref.at[:, below, body], ext_ref.at[:, below, body], sems, 4, sib)
-    swap_corner = remote(ext_ref.at[:, below, edge], ext_ref.at[:, below, edge], sems, 5, sib)
+    to_left = remote(ext.at[:, mine, pl.ds(0, frame)], ext.at[:, mine, edge], sems, 0, left)
+    to_up = remote(ext.at[:, lift, body], ext.at[:, below, body], sems, 1, up)
+    swap_edge = remote(ext.at[:, mine, edge], ext.at[:, mine, edge], sems, 2, sib)
+    corner_up = remote(ext.at[:, lift, edge], ext.at[:, below, edge], sems, 3, up)
+    swap_below = remote(ext.at[:, below, body], ext.at[:, below, body], sems, 4, sib)
+    swap_corner = remote(ext.at[:, below, edge], ext.at[:, below, edge], sems, 5, sib)
+
+    def convert(rows):
+        for plane in range(2):
+            obj_ref[0, plane, rows, body] = field_ref[rows, plane, :].astype(BF16)
+
+    def shifted(rows, start, width):
+        for plane in range(2):
+            value = obj_ref[0, plane, rows, pl.ds(start, width + LANES)].astype(F32)
+            value = pltpu.roll(value, width + LANES - SHIFT, 1)[:, :width]
+            obj_ref[1, plane, rows, pl.ds(start, width)] = value.astype(BF16)
+
+    convert(mine)
 
     @pl.when(has_left)
     def _():
         to_left.start()
 
+    convert(other)
+
     @pl.when(has_up)
     def _():
         to_up.start()
 
-    ext_ref[:, pl.ds(0, tile_r), body] = obj_ref[...]
+    for plane in range(2):
+        planes_ref[plane] = probe_ref[:, plane, :]
+    top, bottom = pl.ds(0, tile_r), pl.ds(tile_r, reach)
+    shifted(top, 0, tile_c - LANES)
+    acc_ref[0] = jnp.zeros(acc_ref.shape[1:], F32)
 
     @pl.when(has_right)
     def _():
         to_left.wait_recv()
+        swap_edge.start()
+
+    acc_ref[1] = jnp.zeros(acc_ref.shape[1:], F32)
+
+    @pl.when(has_right)
+    def _():
+        swap_edge.wait_recv()
 
         @pl.when(has_up)
         def _():
             corner_up.start()
 
-        swap_edge.start()
+        shifted(top, tile_c - LANES, frame)
 
     @pl.when(has_down)
     def _():
         to_up.wait_recv()
         swap_below.start()
+        swap_below.wait_recv()
+        shifted(bottom, 0, tile_c - LANES)
 
     @pl.when(has_right & has_down)
     def _():
         corner_up.wait_recv()
         swap_corner.start()
         swap_corner.wait()
+        shifted(bottom, tile_c - LANES, frame)
 
     @pl.when(has_right)
     def _():
-        swap_edge.wait()
+        swap_edge.wait_send()
 
         @pl.when(has_up)
         def _():
@@ -122,7 +154,7 @@
 
     @pl.when(has_down)
     def _():
-        swap_below.wait()
+        swap_below.wait_send()
 
     @pl.when(has_left)
     def _():
@@ -133,38 +165,38 @@
         to_up.wait_send()
 
 
-def halo(obj, frame, rows_n, cols_n):
-    planes, tile_r, tile_c = obj.shape
+def halo(field, probe, rows_n, cols_n):
+    tile_r, planes, tile_c = field.shape
+    frame = probe.shape[0]
+    shape = (2, planes, tile_r + frame, tile_c + frame)
+    in_vmem = pl.BlockSpec(memory_space=VMEM)
     return pl.pallas_call(
         functools.partial(halo_kernel, rows_n, cols_n),
-        out_shape=jax.ShapeDtypeStruct((planes, tile_r + frame, tile_c + frame), BF16),
-        in_specs=[pl.BlockSpec(memory_space=VMEM)],
-        out_specs=pl.BlockSpec(memory_space=VMEM),
+        out_shape=(
+            jax.ShapeDtypeStruct(shape, BF16),
+            jax.ShapeDtypeStruct((planes, frame, frame), F32),
+            jax.ShapeDtypeStruct(shape, F32),
+        ),
+        in_specs=[in_vmem] * 2,
+        out_specs=(in_vmem,) * 3,
         scratch_shapes=[pltpu.SemaphoreType.DMA((2, 6))],
+        cost_estimate=pl.CostEstimate(flops=0, bytes_accessed=40 << 20, transcendentals=0),
         compiler_params=pltpu.CompilerParams(
-            collective_id=0, has_side_effects=True, vmem_limit_bytes=48 << 20
+            collective_id=0, has_side_effects=True, vmem_limit_bytes=4 << 20
         ),
         name="halo",
-    )(obj)
+    )(field, probe)
 
 
 def frames_kernel(
-    row_ref, col_ref, count_ref, ext_ref, probe_ref, amp_ref, first_ref, second_ref,
-    upd_ref, sum_ref, obj, acc, tall, wide, field,
+    row_ref, col_ref, count_ref, obj, probe_ref, amp_ref, first_ref, second_ref, _zero,
+    acc, sum_ref, tall, wide, field,
 ):
     frame = probe_ref.shape[1]
-    ext_rows, ext_cols = ext_ref.shape[1:]
+    ext_rows, ext_cols = obj.shape[2:]
     top = lax.axis_index("row") * (ext_rows - frame)
     left = lax.axis_index("col") * (ext_cols - frame)
     step = 32
-    for plane in range(2):
-        for row in range(0, ext_rows, 64):
-            rows = pl.ds(row, 64)
-            value = ext_ref[plane, rows, :]
-            obj[0, plane, rows, :] = value
-            moved = pltpu.roll(value.astype(F32), ext_cols - SHIFT, 1)
-            obj[1, plane, rows, :] = moved.astype(BF16)
-    acc[...] = jnp.zeros_like(acc)
     sum_ref[...] = jnp.zeros_like(sum_ref)
 
     def one(slot, carry):
@@ -214,47 +246,46 @@
 
     lax.fori_loop(0, count_ref[0], one, 0)
     for plane in range(2):
-        for row in range(0, ext_rows, 64):
-            rows = pl.ds(row, 64)
-            upd_ref[plane, rows, :] = acc[0, plane, rows, :] + pltpu.roll(
-                acc[1, plane, rows, :], SHIFT, 1
-            )
-
-
-def frames(row_offset, col_offset, counts, ext, probe, amplitudes, first, second):
+        for row in range(0, ext_rows - SHIFT, SHIFT):
+            rows = pl.ds(row, SHIFT)
+            acc[0, plane, rows, :] += pltpu.roll(acc[1, plane, rows, :], SHIFT, 1)
+
+
+def frames(row_offset, col_offset, counts, obj, probe, amplitudes, first, second, acc):
     frame = probe.shape[1]
     in_vmem = pl.BlockSpec(memory_space=VMEM)
     in_smem = pl.BlockSpec(memory_space=pltpu.SMEM)
     return pl.pallas_call(
         frames_kernel,
         out_shape=(
-            jax.ShapeDtypeStruct(ext.shape, F32),
+            jax.ShapeDtypeStruct(acc.shape, F32),
             jax.ShapeDtypeStruct((3, frame, frame), F32),
         ),
-        in_specs=[in_smem] * 3 + [in_vmem] * 5,
+        in_specs=[in_smem] * 3 + [in_vmem] * 6,
         out_specs=(in_vmem, in_vmem),
+        input_output_aliases={8: 0},
         scratch_shapes=[
-            VMEM((2, *ext.shape), BF16),
-            VMEM((2, *ext.shape), F32),
             VMEM((2 * frame, frame), BF16),
             VMEM((frame, 2 * frame), BF16),
             VMEM((frame, 2 * frame), F32),
         ],
-        compiler_params=pltpu.CompilerParams(vmem_limit_bytes=48 << 20),
+        compiler_params=pltpu.CompilerParams(vmem_limit_bytes=10 << 20),
         name="frames",
-    )(row_offset, col_offset, counts, ext, probe, amplitudes, first, second)
+    )(row_offset, col_offset, counts, obj, probe, amplitudes, first, second, acc)
 
 
 def merge_kernel(
-    rows_n, cols_n, with_probe, upd_ref, sum_ref, probe_ref, share_ref, fresh_ref,
-    total, got, from_left, from_up, got_sum, part, col_got, row_part, row_got, sems, psems,
+    rows_n, cols_n, with_probe, acc_ref, sum_ref, probe_ref, field_ref, share_ref, out_ref,
+    fresh_ref, got, total, low_first, to_right, to_down, from_left, from_up,
+    got_sum, part, col_got, row_part, row_got, sems, psems,
 ):
     r = lax.axis_index("row")
     c = lax.axis_index("col")
     m = lax.axis_index("mode")
-    half, tile_c = share_ref.shape[1:]
+    half, _, tile_c = share_ref.shape
     tile_r = 2 * half
     frame = probe_ref.shape[1]
+    upd_ref = acc_ref.at[0]
     has_up, has_down = r > 0, r < rows_n - 1
     has_left, has_right = c > 0, c < cols_n - 1
     sib = {"mode": 1 - m}
@@ -292,12 +323,12 @@
     def joined(index):
         low, cols = pieces[index]
         swaps[index].wait_recv()
-        total[low, :, :, cols] = upd_ref[:, low_mine if low else top_mine, cols] + got[low, :, :, cols]
-
-    corner = remote(total.at[1, :, :, edge], from_left.at[1], sems, 5, right)
-    side = remote(total.at[0, :, :, edge], from_left.at[0], sems, 6, right)
-    fall_mid = remote(total.at[1, :, :, mid_cols], from_up.at[:, :, mid_cols], sems, 7, down)
-    fall_first = remote(total.at[1, :, :, first_cols], from_up.at[:, :, first_cols], sems, 8, down)
+        return upd_ref[:, low_mine if low else top_mine, cols] + got[low, :, :, cols]
+
+    corner = remote(to_right.at[1], from_left.at[1], sems, 5, right)
+    side = remote(to_right.at[0], from_left.at[0], sems, 6, right)
+    fall_mid = remote(to_down.at[:, :, mid_cols], from_up.at[:, :, mid_cols], sems, 7, down)
+    fall_first = remote(to_down.at[:, :, first_cols], from_up.at[:, :, first_cols], sems, 8, down)
 
     if with_probe:
         swap_sum.wait_recv()
@@ -309,25 +340,25 @@
             src = part.at[:, pl.ds(pl.multiple_of(there * col_rows, col_rows), col_rows), :]
             col_copies.append(remote(src, col_got.at[d - 1], psems, d, col_peers[d - 1]))
             col_copies[-1].start()
-    joined(0)
+    to_right[1] = joined(0).astype(BF16)
 
     @pl.when(has_right)
     def _():
         corner.start()
 
-    joined(1)
+    to_down[:, :, mid_cols] = joined(1).astype(BF16)
 
     @pl.when(has_down)
     def _():
         fall_mid.start()
 
-    joined(2)
+    to_right[0] = joined(2).astype(BF16)
 
     @pl.when(has_right)
     def _():
         side.start()
 
-    joined(3)
+    low_first[...] = joined(3)
     base = cols_n
     if with_probe:
         own = part[:, pl.ds(pl.multiple_of(c * col_rows, col_rows), col_rows), :]
@@ -345,10 +376,11 @@
     @pl.when(has_left)
     def _():
         corner.wait_recv()
-        total[1, :, :, first_cols] += from_left[1]
+        low_first[...] += from_left[1].astype(F32)
 
     @pl.when(has_down)
     def _():
+        to_down[:, :, first_cols] = low_first[...].astype(BF16)
         fall_first.start()
 
     peak = probe_ref[0] * probe_ref[0] + probe_ref[1] * probe_ref[1]
@@ -379,12 +411,12 @@
         base += cols_n
     else:
         fresh_ref[...] = jnp.zeros_like(fresh_ref)
-    joined(4)
+    total[...] = joined(4)
 
     @pl.when(has_left)
     def _():
         side.wait_recv()
-        total[0, :, :, first_cols] += from_left[0]
+        total[:, :, first_cols] += from_left[0].astype(F32)
 
     if with_probe:
         for d in range(1, cols_n):
@@ -397,9 +429,10 @@
     def _():
         fall_mid.wait_recv()
         fall_first.wait_recv()
-        total[0, :, :, pl.ds(0, tile_c)] += from_up[...]
-
-    share_ref[...] = total[0, :, :, pl.ds(0, tile_c)] / peak
+        total[...] += from_up[...].astype(F32)
+
+    for plane in range(2):
+        share_ref[:, plane, :] = field_ref[top_mine, plane, :] + total[plane] / peak
 
     for copy in swaps:
         copy.wait_send()
@@ -419,9 +452,12 @@
         for copy in col_copies + row_copies + spread:
             copy.wait_send()
         last.wait()
-
-
-def merge(upd, sums, probe, tile_r, tile_c, rows_n, cols_n, with_probe):
+    for plane in range(2):
+        out_ref[:, plane, :] = fresh_ref[plane]
+
+
+def merge(acc, sums, probe, field, rows_n, cols_n, with_probe):
+    tile_r, _, tile_c = field.shape
     frame = probe.shape[1]
     half = tile_r // 2
     ext_c = tile_c + frame
@@ -435,16 +471,20 @@
     return pl.pallas_call(
         functools.partial(merge_kernel, rows_n, cols_n, with_probe),
         out_shape=(
-            jax.ShapeDtypeStruct((2, half, tile_c), F32),
-            jax.ShapeDtypeStruct((2, frame, frame), F32),
+            jax.ShapeDtypeStruct((half, 2, tile_c), F32),
+            jax.ShapeDtypeStruct((frame, 2, frame), F32),
         ),
-        in_specs=[in_vmem] * 3,
+        in_specs=[in_vmem] * 4,
         out_specs=(in_vmem, in_vmem),
         scratch_shapes=[
+            VMEM((2, frame, frame), F32),
             VMEM((2, 2, half, ext_c), F32),
-            VMEM((2, 2, half, ext_c), F32),
-            VMEM((2, 2, half, frame), F32),
             VMEM((2, half, tile_c), F32),
+            VMEM((2, half, frame), F32),
+            VMEM((2, 2, half, frame), BF16),
+            VMEM((2, half, tile_c), BF16),
+            VMEM((2, 2, half, frame), BF16),
+            VMEM((2, half, tile_c), BF16),
             VMEM((3, sum_rows, frame), F32),
             VMEM((3, sum_rows, frame), F32),
             VMEM((max(1, cols_n - 1), 3, col_rows, frame), F32),
@@ -454,30 +494,26 @@
             pltpu.SemaphoreType.DMA((2, 2 * rows_n + 2 * cols_n + 1)),
         ],
         compiler_params=pltpu.CompilerParams(
-            collective_id=1, has_side_effects=True, vmem_limit_bytes=48 << 20
+            collective_id=1, has_side_effects=True, vmem_limit_bytes=14 << 20
         ),
         name="merge",
-    )(upd, sums, probe)
+    )(acc, sums, probe, field)
 
 
 def body(rows_n, cols_n, object_field, probe_field, amplitudes, row_offset, col_offset, counts):
-    tile_r, _, tile_c = object_field.shape
     frame = probe_field.shape[0]
-    half = tile_r // 2
     first, second = dft_tables(frame)
-    obj = jnp.moveaxis(object_field.astype(BF16), 1, 0)
-    probe = jnp.moveaxis(probe_field, 1, 0)
-    ext = halo(obj, frame, rows_n, cols_n)
-    upd, sums = frames(row_offset, col_offset, counts, ext, probe, amplitudes, first, second)
+    obj, probe, acc = halo(object_field, probe_field, rows_n, cols_n)
+    acc, sums = frames(
+        row_offset, col_offset, counts, obj, probe, amplitudes, first, second, acc
+    )
     with_probe = frame % (2 * rows_n * cols_n * 8) == 0
-    share, fresh = merge(upd, sums, probe, tile_r, tile_c, rows_n, cols_n, with_probe)
-    rows_here = lax.dynamic_slice_in_dim(object_field, lax.axis_index("mode") * half, half, 0)
-    object_new = rows_here + jnp.moveaxis(share, 0, 1)
-    if with_probe:
-        return (object_new, jnp.moveaxis(fresh, 0, 1))
-    sums = lax.psum(sums, ("row", "col", "mode"))
-    fresh = probe + sums[:2] / (sums[2:] + REGULARIZER)
-    return (object_new, jnp.moveaxis(fresh, 0, 1))
+    object_new, fresh = merge(acc, sums, probe, object_field, rows_n, cols_n, with_probe)
+    if not with_probe:
+        sums = lax.psum(sums, ("row", "col", "mode"))
+        fresh = probe + sums[:2] / (sums[2:] + REGULARIZER)
+        fresh = jnp.moveaxis(fresh, 0, 1)
+    return (object_new, fresh)
 
 
 def solution(mesh):

time: 61.2 us -> 56.7 us (0.926)
  Pallas kernels: 52.3 us -> 46.7 us
  local copies, waits for them, and re-layouts: 7.09 us -> 8.28 us
    pallas_call x1, Pallas kernels: 7.23 us -> 2.94 us  [frames(): pl.pallas_call(frames_kernel, out_shape=(jax.ShapeDtypeStruct(acc.shape,...]
    pallas_call x1, Pallas kernels: 35.9 us -> 33.7 us  [merge(): pl.pallas_call(functools.partial(merge_kernel, rows_n, cols_n, with_probe...]
    unnamed x19 -> x18, local copies, waits for them, and re-layouts: 7.09 us -> 8.28 us
    pallas_call x1, Pallas kernels: 9.18 us -> 10 us  [halo(): pl.pallas_call(functools.partial(halo_kernel, rows_n, cols_n), out_shape=...]
where the time goes in v2:
time: 56.7 us; the launch traced here: 56.3 us
  Pallas kernels  46.7 us (82%)
  local copies, waits for them, and re-layouts  8.28 us (15%)
  between operations  1.33 us (2%)
    pallas_call x1, Pallas kernels, merge(): pl.pallas_call(functools.partial(merge_kernel, rows_n, cols_n, with_probe...  33.7 us
    pallas_call x1, Pallas kernels, halo(): pl.pallas_call(functools.partial(halo_kernel, rows_n, cols_n), out_shape=...  10 us
    unnamed x18, local copies, waits for them, and re-layouts  8.28 us
    pallas_call x1, Pallas kernels, frames(): pl.pallas_call(frames_kernel, out_shape=(jax.ShapeDtypeStruct(acc.shape,...  2.94 us

profile of v2, /device:TPU:29, one launch (start us, length us, event | category | flops | bytes accessed | tf_op | source)
XLA Modules:
  0.0 56.3 jit_solution(3937714253996613395)
XLA Ops:
  1.3 0.0 copy-start
  1.3 1.2 %copy-done = f32[256,2,512]{2,1,0:T(2,128)S(1)} copy-done((f32[256,2,512]{2,1,0:T(2,128)S(1)}, f32[256,2,512]{2,1,0:T(2,128)}, u32[]{:S(2)}) %copy-start) | copy-done | bytes 1048600
  2.5 0.0 copy-start.2
  2.5 1.0 %copy-done.2 = f32[256,2,256]{2,1,0:T(2,128)S(1)} copy-done((f32[256,2,256]{2,1,0:T(2,128)S(1)}, f32[256,2,256]{2,1,0:T(2,128)}, u32[]{:S(2)}) %copy-start.2) | copy-done | bytes 524312
  3.5 0.0 copy-start.1
  3.5 10.0 %halo.1 = (bf16[2,2,512,768]{3,2,1,0:T(8,128)(2,1)S(1)}, f32[2,256,256]{2,1,0:T(8,128)S(1)}, f32[2,2,512,768]{3,2,1,0:T(8,128)S(1)}) custom-call(f32[256,2,512]{2,1,0:T(2,128)S(1)} %copy-done, f32[256,2,256]{2,1,0:T(2,128)S(1)} %copy-done.2), custom_call_target="tpu_custom_call" | custom-call | bytes 41943040 | tf_op jit(solution)/shard_map/halo/pallas_call | solution.py:173
  13.6 0.0 copy-start.3
  13.6 1.0 %copy-done.3 = bf16[4,256,256]{2,1,0:T(8,128)(2,1)S(1)} copy-done((bf16[4,256,256]{2,1,0:T(8,128)(2,1)S(1)}, bf16[4,256,256]{2,1,0:T(8,128)(2,1)}, u32[]{:S(2)}) %copy-start.3) | copy-done | bytes 524312
  14.6 0.0 copy-start.4
  14.6 1.0 %copy-done.4 = bf16[512,512]{1,0:T(8,128)(2,1)S(1)} copy-done((bf16[512,512]{1,0:T(8,128)(2,1)S(1)}, bf16[512,512]{1,0:T(8,128)(2,1)}, u32[]{:S(2)}) %copy-start.4) | copy-done | bytes 524312
  15.7 0.0 copy-start.5
  15.7 1.0 %copy-done.5 = bf16[512,512]{1,0:T(8,128)(2,1)S(1)} copy-done((bf16[512,512]{1,0:T(8,128)(2,1)S(1)}, bf16[512,512]{1,0:T(8,128)(2,1)}, u32[]{:S(2)}) %copy-start.5) | copy-done | bytes 524312
  16.7 0.0 copy-start.6
  16.7 0.7 %copy-done.6 = s32[4]{0:T(128)S(1)} copy-done((s32[4]{0:T(128)S(1)}, s32[4]{0:T(128)}, u32[]{:S(2)}) %copy-start.6) | copy-done | bytes 40
  17.4 0.0 copy-start.7
  17.4 0.7 %copy-done.7 = s32[4]{0:T(128)S(1)} copy-done((s32[4]{0:T(128)S(1)}, s32[4]{0:T(128)}, u32[]{:S(2)}) %copy-start.7) | copy-done | bytes 40
  18.0 2.9 %frames.1 = (f32[2,2,512,768]{3,2,1,0:T(8,128)S(1)}, f32[3,256,256]{2,1,0:T(8,128)S(1)}) custom-call(s32[4]{0:T(128)S(1)} %copy-done.6, s32[4]{0:T(128)S(1)} %copy-done.7, s32[1]{0:T(128)S(6)} %copy.14.count_ref, bf16[2,2,512,768]{3,2,1,0:T(8,128)(2,1)S(1)} %get-tuple-element.7.obj, ...), custom_call_target="tpu_custom_call", output_to_operand_aliasing={{0}: (8, {})} | custom-call | tf_op jit(solution)/shard_map/frames/pallas_call | solution.py:258
  21.0 0.0 copy-done.1
  21.0 33.7 %merge.1 = (f32[128,2,512]{2,1,0:T(2,128)S(1)}, f32[256,2,256]{2,1,0:T(2,128)S(1)}) custom-call(f32[2,2,512,768]{3,2,1,0:T(8,128)S(1)} %get-tuple-element.10.acc_ref, f32[3,256,256]{2,1,0:T(8,128)S(1)} %get-tuple-element.11.sum_ref, f32[2,256,256]{2,1,0:T(8,128)S(1)} %get-tuple-element.8.probe_ref, f32[256,2,512]{2,1,0:T(2,128)S(1)} %copy-done.1), custom_call_target="tpu_custom_call" | custom-call | tf_op jit(solution)/shard_map/merge/pallas_call | solution.py:471
  54.7 0.8 %copy.15 = f32[128,2,512]{2,1,0:T(2,128)} copy(f32[128,2,512]{2,1,0:T(2,128)S(1)} %get-tuple-element.14) | data formatting | bytes 1048576
  55.5 0.8 %copy.16 = f32[256,2,256]{2,1,0:T(2,128)} copy(f32[256,2,256]{2,1,0:T(2,128)S(1)} %get-tuple-element.15) | data formatting | bytes 1048576
Async XLA Ops:
  1.3 1.2 %copy-start = (f32[256,2,512]{2,1,0:T(2,128)S(1)}, f32[256,2,512]{2,1,0:T(2,128)}, u32[]{:S(2)}) copy-start(f32[256,2,512]{2,1,0:T(2,128)} %field_ref.3) | copy-start | bytes 3145732
  2.5 1.0 %copy-start.2 = (f32[256,2,256]{2,1,0:T(2,128)S(1)}, f32[256,2,256]{2,1,0:T(2,128)}, u32[]{:S(2)}) copy-start(f32[256,2,256]{2,1,0:T(2,128)} %probe_ref.1) | copy-start | bytes 1572868
  3.5 17.4 %copy-start.1 = (f32[256,2,512]{2,1,0:T(2,128)S(1)}, f32[256,2,512]{2,1,0:T(2,128)}, u32[]{:S(2)}) copy-start(f32[256,2,512]{2,1,0:T(2,128)} %field_ref.3) | copy-start | bytes 3145732
  13.6 1.0 %copy-start.3 = (bf16[4,256,256]{2,1,0:T(8,128)(2,1)S(1)}, bf16[4,256,256]{2,1,0:T(8,128)(2,1)}, u32[]{:S(2)}) copy-start(bf16[4,256,256]{2,1,0:T(8,128)(2,1)} %amp_ref.1) | copy-start | bytes 1572868
  14.6 1.0 %copy-start.4 = (bf16[512,512]{1,0:T(8,128)(2,1)S(1)}, bf16[512,512]{1,0:T(8,128)(2,1)}, u32[]{:S(2)}) copy-start(bf16[512,512]{1,0:T(8,128)(2,1)} %constant.5.clone.second_ref) | copy-start | bytes 1572868
  15.7 1.0 %copy-start.5 = (bf16[512,512]{1,0:T(8,128)(2,1)S(1)}, bf16[512,512]{1,0:T(8,128)(2,1)}, u32[]{:S(2)}) copy-start(bf16[512,512]{1,0:T(8,128)(2,1)} %constant.4.clone.first_ref) | copy-start | bytes 1572868
  16.7 0.7 %copy-start.6 = (s32[4]{0:T(128)S(1)}, s32[4]{0:T(128)}, u32[]{:S(2)}) copy-start(s32[4]{0:T(128)} %row_ref.1) | copy-start | bytes 52
  17.4 0.7 %copy-start.7 = (s32[4]{0:T(128)S(1)}, s32[4]{0:T(128)}, u32[]{:S(2)}) copy-start(s32[4]{0:T(128)} %col_ref.1) | copy-start | bytes 52

commit v3 on v2

--- a/solution.py
+++ b/solution.py
@@ -56,7 +56,16 @@
     )
 
 
-def halo_kernel(rows_n, cols_n, field_ref, probe_ref, obj_ref, planes_ref, acc_ref, sems):
+def halo_kernel(rows_n, cols_n, count, *refs):
+    field_hbm, probe_hbm = refs[:2]
+    extras = refs[2 : 2 + count]
+    obj_ref, planes_ref, acc_ref = refs[2 + count : 5 + count]
+    landed = refs[5 + count : 5 + 2 * count]
+    field_ref, probe_ref, sems, local = refs[5 + 2 * count :]
+    pairs = [(field_hbm, field_ref), (probe_hbm, probe_ref), *zip(extras, landed)]
+    fetches = [pltpu.make_async_copy(a, b, local.at[i]) for i, (a, b) in enumerate(pairs)]
+    for fetch in fetches:
+        fetch.start()
     r = lax.axis_index("row")
     c = lax.axis_index("col")
     m = lax.axis_index("mode")
@@ -95,6 +104,7 @@
             value = pltpu.roll(value, width + LANES - SHIFT, 1)[:, :width]
             obj_ref[1, plane, rows, pl.ds(start, width)] = value.astype(BF16)
 
+    fetches[0].wait()
     convert(mine)
 
     @pl.when(has_left)
@@ -107,6 +117,7 @@
     def _():
         to_up.start()
 
+    fetches[1].wait()
     for plane in range(2):
         planes_ref[plane] = probe_ref[:, plane, :]
     top, bottom = pl.ds(0, tile_r), pl.ds(tile_r, reach)
@@ -164,28 +175,37 @@
     def _():
         to_up.wait_send()
 
-
-def halo(field, probe, rows_n, cols_n):
+    for fetch in fetches[2:]:
+        fetch.wait()
+
+
+def halo(field, probe, extras, rows_n, cols_n):
     tile_r, planes, tile_c = field.shape
     frame = probe.shape[0]
     shape = (2, planes, tile_r + frame, tile_c + frame)
     in_vmem = pl.BlockSpec(memory_space=VMEM)
     return pl.pallas_call(
-        functools.partial(halo_kernel, rows_n, cols_n),
+        functools.partial(halo_kernel, rows_n, cols_n, len(extras)),
         out_shape=(
             jax.ShapeDtypeStruct(shape, BF16),
             jax.ShapeDtypeStruct((planes, frame, frame), F32),
             jax.ShapeDtypeStruct(shape, F32),
+            *(jax.ShapeDtypeStruct(x.shape, x.dtype) for x in extras),
         ),
-        in_specs=[in_vmem] * 2,
-        out_specs=(in_vmem,) * 3,
-        scratch_shapes=[pltpu.SemaphoreType.DMA((2, 6))],
+        in_specs=[pl.BlockSpec(memory_space=pltpu.HBM)] * (2 + len(extras)),
+        out_specs=(in_vmem,) * (3 + len(extras)),
+        scratch_shapes=[
+            VMEM(field.shape, F32),
+            VMEM(probe.shape, F32),
+            pltpu.SemaphoreType.DMA((2, 6)),
+            pltpu.SemaphoreType.DMA((2 + len(extras),)),
+        ],
         cost_estimate=pl.CostEstimate(flops=0, bytes_accessed=40 << 20, transcendentals=0),
         compiler_params=pltpu.CompilerParams(
-            collective_id=0, has_side_effects=True, vmem_limit_bytes=4 << 20
+            collective_id=0, has_side_effects=True, vmem_limit_bytes=8 << 20
         ),
         name="halo",
-    )(field, probe)
+    )(*(pltpu.with_memory_space_constraint(x, pltpu.HBM) for x in (field, probe, *extras)))
 
 
 def frames_kernel(
@@ -276,8 +296,8 @@
 
 def merge_kernel(
     rows_n, cols_n, with_probe, acc_ref, sum_ref, probe_ref, field_ref, share_ref, out_ref,
-    fresh_ref, got, total, low_first, to_right, to_down, from_left, from_up,
-    got_sum, part, col_got, row_part, row_got, sems, psems,
+    fresh_ref, got, total, to_right, to_down, from_left, from_up,
+    got_sum, part, col_got, row_part, row_got, sems, psems, asems,
 ):
     r = lax.axis_index("row")
     c = lax.axis_index("col")
@@ -285,9 +305,11 @@
     half, _, tile_c = share_ref.shape
     tile_r = 2 * half
     frame = probe_ref.shape[1]
+    near = frame - SHIFT - half
     upd_ref = acc_ref.at[0]
     has_up, has_down = r > 0, r < rows_n - 1
     has_left, has_right = c > 0, c < cols_n - 1
+    whole = m == 0
     sib = {"mode": 1 - m}
     up, down = {"row": r - 1}, {"row": r + 1}
     left, right = {"col": c - 1}, {"col": c + 1}
@@ -304,35 +326,26 @@
 
     top_mine, low_mine = block(m, 0), block(m, tile_r)
     top_sib, low_sib = block(1 - m, 0), block(1 - m, tile_r)
-    first_cols, mid_cols, edge = pl.ds(0, frame), pl.ds(frame, tile_c - frame), pl.ds(tile_c, frame)
-    pieces = [(1, edge), (1, mid_cols), (0, edge), (1, first_cols), (0, pl.ds(0, tile_c))]
+    first_cols, body, edge = pl.ds(0, frame), pl.ds(0, tile_c), pl.ds(tile_c, frame)
+    near_rows, far_rows = pl.ds(0, near), pl.ds(near, half - near)
     if with_probe:
         sum_rows = frame // 2
         col_rows = sum_rows // cols_n
         row_rows = col_rows // rows_n
-        mine_at = m * sum_rows
         give = sum_ref.at[:, pl.ds(pl.multiple_of((1 - m) * sum_rows, sum_rows), sum_rows), :]
         swap_sum = remote(give, got_sum, psems, 0, sib)
         swap_sum.start()
-    swaps = []
-    for slot, (low, cols) in enumerate(pieces):
-        src = upd_ref.at[:, low_sib if low else top_sib, cols]
-        swaps.append(remote(src, got.at[low, :, :, cols], sems, slot, sib))
-        swaps[-1].start()
-
-    def joined(index):
-        low, cols = pieces[index]
-        swaps[index].wait_recv()
-        return upd_ref[:, low_mine if low else top_mine, cols] + got[low, :, :, cols]
-
-    corner = remote(to_right.at[1], from_left.at[1], sems, 5, right)
-    side = remote(to_right.at[0], from_left.at[0], sems, 6, right)
-    fall_mid = remote(to_down.at[:, :, mid_cols], from_up.at[:, :, mid_cols], sems, 7, down)
-    fall_first = remote(to_down.at[:, :, first_cols], from_up.at[:, :, first_cols], sems, 8, down)
+    swap_low = remote(upd_ref.at[:, low_sib, :], got.at[1], sems, 0, sib)
+    swap_low.start()
+    swap_top = remote(upd_ref.at[:, top_sib, :], got.at[0], sems, 1, sib)
+    swap_top.start()
+    fall_near = remote(to_down.at[:, near_rows, :], from_up.at[:, near_rows, :], sems, 2, down)
+    fall_far = remote(to_down.at[:, far_rows, :], from_up.at[:, far_rows, :], sems, 3, down)
+    side = remote(to_right, from_left, sems, 4, right)
 
     if with_probe:
         swap_sum.wait_recv()
-        at = pl.ds(pl.multiple_of(mine_at, sum_rows), sum_rows)
+        at = pl.ds(pl.multiple_of(m * sum_rows, sum_rows), sum_rows)
         part[...] = sum_ref[:, at, :] + got_sum[...]
         col_copies = []
         for d in range(1, cols_n):
@@ -340,26 +353,21 @@
             src = part.at[:, pl.ds(pl.multiple_of(there * col_rows, col_rows), col_rows), :]
             col_copies.append(remote(src, col_got.at[d - 1], psems, d, col_peers[d - 1]))
             col_copies[-1].start()
-    to_right[1] = joined(0).astype(BF16)
-
-    @pl.when(has_right)
-    def _():
-        corner.start()
-
-    to_down[:, :, mid_cols] = joined(1).astype(BF16)
+    swap_low.wait_recv()
+    to_down[...] = (upd_ref[:, low_mine, :] + got[1]).astype(BF16)
 
     @pl.when(has_down)
     def _():
-        fall_mid.start()
-
-    to_right[0] = joined(2).astype(BF16)
-
-    @pl.when(has_right)
-    def _():
-        side.start()
-
-    low_first[...] = joined(3)
-    base = cols_n
+        fall_near.start()
+
+        @pl.when(whole)
+        def _():
+            fall_far.start()
+
+    swap_top.wait_recv()
+    total[...] = upd_ref[:, top_mine, :] + got[0]
+    peak = probe_ref[0] * probe_ref[0] + probe_ref[1] * probe_ref[1]
+    peak = jnp.max(peak, keepdims=True) + EPSILON
     if with_probe:
         own = part[:, pl.ds(pl.multiple_of(c * col_rows, col_rows), col_rows), :]
         for d in range(1, cols_n):
@@ -370,90 +378,103 @@
         for d in range(1, rows_n):
             there = lax.rem(r + d, rows_n)
             src = row_part.at[:, pl.ds(pl.multiple_of(there * row_rows, row_rows), row_rows), :]
-            row_copies.append(remote(src, row_got.at[d - 1], psems, base + d, row_peers[d - 1]))
+            row_copies.append(remote(src, row_got.at[d - 1], psems, cols_n + d, row_peers[d - 1]))
             row_copies[-1].start()
 
-    @pl.when(has_left)
-    def _():
-        corner.wait_recv()
-        low_first[...] += from_left[1].astype(F32)
-
-    @pl.when(has_down)
-    def _():
-        to_down[:, :, first_cols] = low_first[...].astype(BF16)
-        fall_first.start()
-
-    peak = probe_ref[0] * probe_ref[0] + probe_ref[1] * probe_ref[1]
-    peak = jnp.max(peak, keepdims=True) + EPSILON
-    base += rows_n
+    @pl.when(has_up)
+    def _():
+        fall_near.wait_recv()
+        total[:, near_rows, :] += from_up[:, near_rows, :].astype(F32)
+
+        @pl.when(whole)
+        def _():
+            fall_far.wait_recv()
+            total[:, far_rows, :] += from_up[:, far_rows, :].astype(F32)
+
+    @pl.when(has_right)
+    def _():
+        to_right[...] = total[:, :, edge].astype(BF16)
+        side.start()
+
+    spread = []
     if with_probe:
         own = row_part[:, pl.ds(pl.multiple_of(r * row_rows, row_rows), row_rows), :]
         for d in range(1, rows_n):
             row_copies[d - 1].wait_recv()
             own = own + row_got[d - 1]
         weight = own[2] + REGULARIZER
-        start = mine_at + c * col_rows
-        shard = pl.ds(pl.multiple_of(start + r * row_rows, row_rows), row_rows)
-        fresh_ref[0, shard, :] = probe_ref[0, shard, :] + own[0] / weight
-        fresh_ref[1, shard, :] = probe_ref[1, shard, :] + own[1] / weight
-        spread = []
+
+        def shard(row):
+            start = m * sum_rows + c * col_rows + row * row_rows
+            return pl.ds(pl.multiple_of(start, row_rows), row_rows)
+
+        here = shard(r)
+        fresh_ref[0, here, :] = probe_ref[0, here, :] + own[0] / weight
+        fresh_ref[1, here, :] = probe_ref[1, here, :] + own[1] / weight
+
+        def pass_on(back):
+            ref = fresh_ref.at[:, shard(lax.rem(r + rows_n - back, rows_n)), :]
+            for d in range(1, cols_n):
+                slot = rows_n + back * cols_n + d
+                copy = remote(ref, ref, asems, slot, col_peers[d - 1])
+                copy.start()
+                crossings.append(copy)
+
+        crossings = []
+        ref = fresh_ref.at[:, here, :]
         for d in range(1, rows_n):
-            ref = fresh_ref.at[:, shard, :]
-            spread.append(remote(ref, ref, psems, base + d, row_peers[d - 1]))
+            spread.append(remote(ref, ref, asems, d, row_peers[d - 1]))
             spread[-1].start()
-        base += rows_n
+        pass_on(0)
         for d in range(1, rows_n):
             spread[d - 1].wait_recv()
-        ref = fresh_ref.at[:, pl.ds(pl.multiple_of(start, col_rows), col_rows), :]
-        for d in range(1, cols_n):
-            spread.append(remote(ref, ref, psems, base + d, col_peers[d - 1]))
-            spread[-1].start()
-        base += cols_n
+            pass_on(d)
     else:
         fresh_ref[...] = jnp.zeros_like(fresh_ref)
-    total[...] = joined(4)
 
     @pl.when(has_left)
     def _():
         side.wait_recv()
-        total[:, :, first_cols] += from_left[0].astype(F32)
-
-    if with_probe:
-        for d in range(1, cols_n):
-            spread[rows_n - 1 + d - 1].wait_recv()
-        ref = fresh_ref.at[:, pl.ds(pl.multiple_of(mine_at, sum_rows), sum_rows), :]
-        last = remote(ref, ref, psems, base, sib)
+        total[:, :, first_cols] += from_left[...].astype(F32)
+
+    for plane in range(2):
+        share_ref[:, plane, :] = field_ref[top_mine, plane, :] + total[plane, :, body] / peak
+
+    if with_probe:
+        for copy in crossings:
+            copy.wait_recv()
+        ref = fresh_ref.at[:, at, :]
+        last = remote(ref, ref, asems, 0, sib)
         last.start()
-
-    @pl.when(has_up)
-    def _():
-        fall_mid.wait_recv()
-        fall_first.wait_recv()
-        total[...] += from_up[...].astype(F32)
-
-    for plane in range(2):
-        share_ref[:, plane, :] = field_ref[top_mine, plane, :] + total[plane] / peak
-
-    for copy in swaps:
-        copy.wait_send()
+        for plane in range(2):
+            out_ref[at, plane, :] = fresh_ref[plane, at, :]
+
+    swap_low.wait_send()
+    swap_top.wait_send()
 
     @pl.when(has_right)
     def _():
-        corner.wait_send()
         side.wait_send()
 
     @pl.when(has_down)
     def _():
-        fall_mid.wait_send()
-        fall_first.wait_send()
+        fall_near.wait_send()
+
+        @pl.when(whole)
+        def _():
+            fall_far.wait_send()
 
     if with_probe:
         swap_sum.wait_send()
-        for copy in col_copies + row_copies + spread:
+        for copy in col_copies + row_copies + spread + crossings:
             copy.wait_send()
         last.wait()
-    for plane in range(2):
-        out_ref[:, plane, :] = fresh_ref[plane]
+        off = pl.ds(pl.multiple_of((1 - m) * sum_rows, sum_rows), sum_rows)
+        for plane in range(2):
+            out_ref[off, plane, :] = fresh_ref[plane, off, :]
+    else:
+        for plane in range(2):
+            out_ref[:, plane, :] = fresh_ref[plane]
 
 
 def merge(acc, sums, probe, field, rows_n, cols_n, with_probe):
@@ -479,19 +500,19 @@
         scratch_shapes=[
             VMEM((2, frame, frame), F32),
             VMEM((2, 2, half, ext_c), F32),
-            VMEM((2, half, tile_c), F32),
-            VMEM((2, half, frame), F32),
-            VMEM((2, 2, half, frame), BF16),
-            VMEM((2, half, tile_c), BF16),
-            VMEM((2, 2, half, frame), BF16),
-            VMEM((2, half, tile_c), BF16),
+            VMEM((2, half, ext_c), F32),
+            VMEM((2, half, frame), BF16),
+            VMEM((2, half, ext_c), BF16),
+            VMEM((2, half, frame), BF16),
+            VMEM((2, half, ext_c), BF16),
             VMEM((3, sum_rows, frame), F32),
             VMEM((3, sum_rows, frame), F32),
             VMEM((max(1, cols_n - 1), 3, col_rows, frame), F32),
             VMEM((3, col_rows, frame), F32),
             VMEM((max(1, rows_n - 1), 3, row_rows, frame), F32),
-            pltpu.SemaphoreType.DMA((2, 9)),
-            pltpu.SemaphoreType.DMA((2, 2 * rows_n + 2 * cols_n + 1)),
+            pltpu.SemaphoreType.DMA((2, 5)),
+            pltpu.SemaphoreType.DMA((2, rows_n + cols_n)),
+            pltpu.SemaphoreType.DMA((2, rows_n + rows_n * cols_n)),
         ],
         compiler_params=pltpu.CompilerParams(
             collective_id=1, has_side_effects=True, vmem_limit_bytes=14 << 20
@@ -503,10 +524,10 @@
 def body(rows_n, cols_n, object_field, probe_field, amplitudes, row_offset, col_offset, counts):
     frame = probe_field.shape[0]
     first, second = dft_tables(frame)
-    obj, probe, acc = halo(object_field, probe_field, rows_n, cols_n)
-    acc, sums = frames(
-        row_offset, col_offset, counts, obj, probe, amplitudes, first, second, acc
-    )
+    extras = (row_offset, col_offset, amplitudes, first, second)
+    obj, probe, acc, *extras = halo(object_field, probe_field, extras, rows_n, cols_n)
+    rows, cols, amplitudes, first, second = extras
+    acc, sums = frames(rows, cols, counts, obj, probe, amplitudes, first, second, acc)
     with_probe = frame % (2 * rows_n * cols_n * 8) == 0
     object_new, fresh = merge(acc, sums, probe, object_field, rows_n, cols_n, with_probe)
     if not with_probe:

time: 56.7 us -> 51.9 us (0.915)
  the two profiles are of different devices: /device:TPU:29 before, /device:TPU:7 now
where the time goes in v3:
time: 51.9 us; the launch traced here: 50.9 us
  Pallas kernels  48 us (92%)
  local copies, waits for them, and re-layouts  1.59 us (3%)
  between operations  1.32 us (3%)
    pallas_call x1, Pallas kernels, merge(): pl.pallas_call(functools.partial(merge_kernel, rows_n, cols_n, with_probe...  34.2 us
    pallas_call x1, Pallas kernels, halo(): pl.pallas_call(functools.partial(halo_kernel, rows_n, cols_n, len(extras)...  10.9 us
    pallas_call x1, Pallas kernels, frames(): pl.pallas_call(frames_kernel, out_shape=(jax.ShapeDtypeStruct(acc.shape,...  2.94 us
    unnamed x4, local copies, waits for them, and re-layouts  1.59 us

profile of v3, /device:TPU:7, one launch (start us, length us, event | category | flops | bytes accessed | tf_op | source)
XLA Modules:
  0.0 50.9 jit_solution(1154094337397960829)
XLA Ops:
  1.3 10.9 %halo.1 = (bf16[2,2,512,768]{3,2,1,0:T(8,128)(2,1)S(1)}, f32[2,256,256]{2,1,0:T(8,128)S(1)}, f32[2,2,512,768]{3,2,1,0:T(8,128)S(1)}, s32[4]{0:T(128)S(1)}, s32[4...) custom-call(f32[256,2,512]{2,1,0:T(2,128)} %field_ref.1, ...), custom_call_target="tpu_custom_call" | custom-call | bytes 41943040 | tf_op jit(solution)/shard_map/halo/pallas_call | solution.py:187
  12.1 0.0 copy-start
  12.2 2.9 %frames.1 = (f32[2,2,512,768]{3,2,1,0:T(8,128)S(1)}, f32[3,256,256]{2,1,0:T(8,128)S(1)}) custom-call(s32[4]{0:T(128)S(1)} %get-tuple-element.12.row_ref, s32[4]{0:T(128)S(1)} %get-tuple-element.13.col_ref, s32[1]{0:T(128)S(6)} %copy.14.count_ref, bf16[2,2,512,768]{3,2,1,0:T(8,128)(2,1)S(1)} %get-tuple-element.14.obj, ...), custom_call_target="tpu_custom_call", output_to_operand_aliasing={{0}: (8, {})} | custom-call | tf_op jit(solution)/shard_map/frames/pallas_call | solution.py:278
  15.1 0.0 copy-done
  15.1 34.2 %merge.1 = (f32[128,2,512]{2,1,0:T(2,128)S(1)}, f32[256,2,256]{2,1,0:T(2,128)S(1)}) custom-call(f32[2,2,512,768]{3,2,1,0:T(8,128)S(1)} %get-tuple-element.20.acc_ref, f32[3,256,256]{2,1,0:T(8,128)S(1)} %get-tuple-element.21.sum_ref, f32[2,256,256]{2,1,0:T(8,128)S(1)} %get-tuple-element.15.probe_ref, f32[256,2,512]{2,1,0:T(2,128)S(1)} %copy-done), custom_call_target="tpu_custom_call" | custom-call | tf_op jit(solution)/shard_map/merge/pallas_call | solution.py:492
  49.3 0.8 %copy.15 = f32[128,2,512]{2,1,0:T(2,128)} copy(f32[128,2,512]{2,1,0:T(2,128)S(1)} %get-tuple-element.24) | data formatting | bytes 1048576
  50.1 0.8 %copy.16 = f32[256,2,256]{2,1,0:T(2,128)} copy(f32[256,2,256]{2,1,0:T(2,128)S(1)} %get-tuple-element.25) | data formatting | bytes 1048576
Async XLA Ops:
  12.1 3.0 %copy-start = (f32[256,2,512]{2,1,0:T(2,128)S(1)}, f32[256,2,512]{2,1,0:T(2,128)}, u32[]{:S(2)}) copy-start(f32[256,2,512]{2,1,0:T(2,128)} %field_ref.1) | copy-start | bytes 3145732
